TPU v7x, 512 devices: a whole 4x8x8 slice. The times are simulated.
512 devices in a mesh: dp: 32 (over x, y_hi, core), fsdp: 16 (over y_lo, z).
Axes of the slice: x: 4, y: 8 (y_hi: 4, y_lo: 2; y = y_hi * 2 + y_lo), z: 8, core: 2. Of those that a mesh axis runs over, the one named last changes fastest.
Arguments:
- hidden: bfloat16 [4, 2048, 16, 4096], P(None, 'dp', 'fsdp'), may hold values from -6 to 6
- frozen_query_rows: bfloat16 [4, 2048, 16, 2048], P(None, 'dp', 'fsdp'), may hold values from -10 to 10
- output_gradient: bfloat16 [4, 2048, 16, 2048], P(None, 'dp', 'fsdp'), may hold values from -6 to 6
- token_log_ratio: float32 [4, 2048, 16], P(None, 'dp', 'fsdp'), may hold values from -0.15625 to 0.15625
- lengths: int32 [4], replicated, may hold values from 1 to 32768, as said below
- response_win_probability: float32 [4], replicated, may hold values from 0.05 to 0.95
- cached_prompt_keys: bfloat16 [1024, 512], P('fsdp'), may hold values from -7.5 to 7.5
- cached_prompt_values: bfloat16 [1024, 512], P('fsdp'), may hold values from -6 to 6
- adapter_down_factor: bfloat16 [4096, 64], P('fsdp'), may hold values from -0.09375 to 0.09375
- adapter_up_factor: bfloat16 [64, 2048], P(None, 'fsdp'), may hold values from -0.125 to 0.125
- attention_norm_gain: bfloat16 [4096], P('fsdp'), may hold values from 0.5 to 1.5
Outputs:
- grad_down: float32 [4096, 64], P('fsdp')
- grad_up: float32 [64, 2048], P(None, 'fsdp')
- seq_ratio: float32 [4], replicated
Inputs may be any that keep to these rules, and one draw needn't show every extreme that they name: The lengths sum to 65472 and the longest is exactly 32768.
All inputs are finite; a program needn't handle non-finite values.
Results may differ from a plain program's by a relative error of at most 0.012.
Values may be sent and summed in bfloat16 or wider, within the bound.
A program may use at most 128 MiB of HBM per device.

v0:
```python
import math
import jax
import jax.numpy as jnp
from jax import lax
from jax.sharding import PartitionSpec as P

HEAD_SIZE = 128
QUERY_HEADS = 16
KEY_VALUE_HEADS = 4
target_scale = 1.0
norm_epsilon = 1e-05


def attend(query_vectors, cotangent, key_rows, value_rows):
    row_count = query_vectors.shape[0]
    queries_per_group = QUERY_HEADS // KEY_VALUE_HEADS
    score_scale = 1.0 / math.sqrt(HEAD_SIZE)
    pieces = []
    for shared_key_head in range(KEY_VALUE_HEADS):
        head_start = shared_key_head * queries_per_group * HEAD_SIZE
        head_stop = head_start + queries_per_group * HEAD_SIZE
        head_query = query_vectors[:, head_start:head_stop].reshape(
            row_count, queries_per_group, HEAD_SIZE
        )
        head_grad = cotangent[:, head_start:head_stop].reshape(
            row_count, queries_per_group, HEAD_SIZE
        )
        head_key = key_rows[:, shared_key_head * HEAD_SIZE : (shared_key_head + 1) * HEAD_SIZE]
        head_value = value_rows[:, shared_key_head * HEAD_SIZE : (shared_key_head + 1) * HEAD_SIZE]
        scores = (
            jnp.einsum("nhd,jd->nhj", head_query, head_key, preferred_element_type=jnp.float32)
            * score_scale
        )
        row_top = jnp.max(scores, axis=2, keepdims=True)
        exponent = jnp.exp(scores - row_top)
        row_total = jnp.sum(exponent, axis=2, keepdims=True)
        weights = exponent.astype(jnp.bfloat16)
        mixed_out = (
            jnp.einsum("nhj,jd->nhd", weights, head_value, preferred_element_type=jnp.float32)
            / row_total
        )
        inner_prod = jnp.sum(head_grad.astype(jnp.float32) * mixed_out, axis=2, keepdims=True)
        grad_prob = jnp.einsum(
            "nhd,jd->nhj", head_grad, head_value, preferred_element_type=jnp.float32
        )
        grad_score = (weights.astype(jnp.float32) / row_total * (grad_prob - inner_prod)).astype(
            jnp.bfloat16
        )
        query_gradient = (
            jnp.einsum("nhj,jd->nhd", grad_score, head_key, preferred_element_type=jnp.float32)
            * score_scale
        )
        pieces.append(query_gradient.reshape(row_count, queries_per_group * HEAD_SIZE))
    return jnp.concatenate(pieces, axis=1).astype(jnp.bfloat16)


def body(
    hidden,
    frozen_query_rows,
    output_gradient,
    token_log_ratio,
    lengths,
    response_win_probability,
    cached_prompt_keys,
    cached_prompt_values,
    adapter_down_factor,
    adapter_up_factor,
    attention_norm_gain,
):
    fsdp_count = lax.axis_size("fsdp")
    dp_index = lax.axis_index("dp")
    fsdp_index = lax.axis_index("fsdp")
    responses, per_device, single, feature_count = hidden.shape
    home_rows = responses * per_device
    local_rows = jnp.arange(per_device, dtype=jnp.int32)
    position = (dp_index * per_device + local_rows) * fsdp_count + fsdp_index
    is_valid = position[None, :] < lengths[:, None]
    partial_value = jnp.sum(jnp.where(is_valid, token_log_ratio[:, :, 0], 0.0), axis=1)
    seq_ratio = lax.psum(partial_value, ("dp", "fsdp"))
    weighting = 2.0 * (seq_ratio - target_scale * (response_win_probability - 0.5)) / responses
    down_full, up_full, gain_full = (
        lax.all_gather(adapter_down_factor, "fsdp", axis=0, tiled=True),
        lax.all_gather(adapter_up_factor, "fsdp", axis=1, tiled=True),
        lax.all_gather(attention_norm_gain, "fsdp", axis=0, tiled=True),
    )
    key_rows, value_rows = (
        lax.all_gather(cached_prompt_keys, "fsdp", axis=0, tiled=True),
        lax.all_gather(cached_prompt_values, "fsdp", axis=0, tiled=True),
    )
    widened = hidden.reshape(home_rows, feature_count).astype(jnp.float32)
    inverse = lax.rsqrt(jnp.mean(widened * widened, axis=1, keepdims=True) + norm_epsilon)
    normed_input = (widened * inverse * gain_full.astype(jnp.float32)).astype(jnp.bfloat16)
    lowrank_hidden = jnp.dot(normed_input, down_full, preferred_element_type=jnp.float32).astype(
        jnp.bfloat16
    )
    row_mask = is_valid.reshape(home_rows)
    row_coef = jnp.repeat(weighting, per_device)
    base_rows = frozen_query_rows.reshape(home_rows, -1)
    cotangent = jnp.where(
        row_mask[:, None],
        row_coef[:, None] * output_gradient.reshape(home_rows, -1).astype(jnp.float32),
        0.0,
    ).astype(jnp.bfloat16)
    query_vectors = (
        base_rows.astype(jnp.float32)
        + jnp.dot(lowrank_hidden, up_full, preferred_element_type=jnp.float32)
    ).astype(jnp.bfloat16)
    query_gradient = attend(query_vectors, cotangent, key_rows, value_rows)
    up_term = jnp.dot(lowrank_hidden.T, query_gradient, preferred_element_type=jnp.float32)
    gradient_lowrank = jnp.dot(
        query_gradient, up_full.T, preferred_element_type=jnp.float32
    ).astype(jnp.bfloat16)
    down_term = jnp.dot(normed_input.T, gradient_lowrank, preferred_element_type=jnp.float32)
    down_sum, up_sum = lax.psum((down_term, up_term), ("dp", "fsdp"))
    down_factor_part = adapter_down_factor.shape[0]
    up_factor_part = adapter_up_factor.shape[1]
    grad_down = lax.dynamic_slice_in_dim(
        down_sum, fsdp_index * down_factor_part, down_factor_part, 0
    )
    grad_up = lax.dynamic_slice_in_dim(up_sum, fsdp_index * up_factor_part, up_factor_part, 1)
    return (grad_down, grad_up, seq_ratio)


def solution(mesh):
    in_specs = (
        P(None, "dp", "fsdp", None),
        P(None, "dp", "fsdp", None),
        P(None, "dp", "fsdp", None),
        P(None, "dp", "fsdp"),
        P(),
        P(),
        P("fsdp", None),
        P("fsdp", None),
        P("fsdp", None),
        P(None, "fsdp"),
        P("fsdp"),
    )
    out_specs = (P("fsdp", None), P(None, "fsdp"), P())
    return jax.shard_map(body, mesh=mesh, in_specs=in_specs, out_specs=out_specs, check_vma=False)
```

profile of v0, /device:TPU:17, one launch (start us, length us, event | category | flops | bytes accessed | tf_op | source)
XLA Modules:
  0.0 574.0 jit_solution(2248930495816452318)
XLA Ops:
  9.6 105.0 %psum.21 = f32[4]{0:T(128)S(1)} all-reduce(f32[4]{0:T(128)S(1)} %get-tuple-element.5), channel_id=1, replica_groups=mesh['dp'=32,'fsdp'=16] {'dp','fsdp'}, use_global_device_ids=true, to_apply=%region_4.5 | all-reduce | flops 4 | bytes 32 | tf_op jit(solution)/shard_map/psum | solution.py:79
  116.1 2.1 multiply_reduce_fusion
  118.3 24.8 %all-gather = bf16[16,1,256]{2,1,0:T(2,128)(2,1)S(1)} all-gather(bf16[1,1,256]{2,1,0:T(2,128)(2,1)S(1)} %reshape.122), channel_id=1, replica_groups=mesh['dp'=32,'fsdp'=16] {'fsdp'}, dimensions={0}, use_global_device_ids=true | all-gather | bytes 8704 | tf_op jit(solution)/shard_map/all_gather | solution.py:84
  143.1 2.2 fusion.1
  152.9 24.4 %all_gather.17 = bf16[64,2048]{1,0:T(8,128)(2,1)S(1)} all-gather(bf16[64,128]{1,0:T(8,128)(2,1)S(1)} %copy-done.17), channel_id=1, replica_groups=mesh['dp'=32,'fsdp'=16] {'fsdp'}, dimensions={1}, use_global_device_ids=true | all-gather | bytes 278528 | tf_op jit(solution)/shard_map/all_gather | solution.py:83
  177.3 27.5 %all_gather.16 = bf16[4096,64]{0,1:T(8,128)(2,1)S(1)} all-gather(bf16[256,64]{0,1:T(8,128)(2,1)S(1)} %copy-done.16), channel_id=1, replica_groups=mesh['dp'=32,'fsdp'=16] {'fsdp'}, dimensions={0}, use_global_device_ids=true | all-gather | bytes 557056 | tf_op jit(solution)/shard_map/all_gather | solution.py:82
  208.8 2.0 copy-done
  211.9 3.0 fusion.39
  216.4 1.9 multiply_reduce_fusion.1
  218.3 1.9 copy-done.1
  222.0 3.1 fusion.30
  226.6 1.8 multiply_reduce_fusion.2
  228.4 2.0 copy-done.2
  232.1 3.1 fusion.33
  236.6 1.8 multiply_reduce_fusion.3
  238.4 1.9 copy-done.3
  242.3 3.1 fusion.36
  246.9 4.8 fusion.21
  251.7 4.8 fusion.24
  256.5 4.8 fusion.23
  261.3 4.8 fusion.22
  266.2 3.6 fusion.25
  269.8 2.2 fusion.70
  272.0 292.6 %all-reduce.3.cloned.1.call-done = (f32[4096,64]{0,1:T(8,128)}, f32[64,2048]{1,0:T(8,128)}) async-done(((f32[4096,64]{0,1:T(8,128)}, f32[64,2048]{1,0:T(8,128)}), (f32[4096,64]{0,1:T(8,128)}, f32[64,2048]{1,0:T(8,128)})) %all-reduce.3.cloned.1.call-update) | async-done | bytes 1572880 | tf_op jit(solution)/shard_map/psum | solution.py:114
  (106 shorter events, 30.8 us)
Async XLA Ops:
  7.2 138.2 %copy-start.6 = (bf16[4,64,1,2048]{3,1,2,0:T(8,128)(2,1)S(1)}, bf16[4,64,1,2048]{3,1,2,0:T(8,128)(2,1)}, u32[]{:S(2)}) copy-start(bf16[4,64,1,2048]{3,1,2,0:T(8,128)(2,1)} %param.13) | copy-start | bytes 3145732
  7.2 199.9 %all-gather.4.cloned.1.call-start = ((), (), s32[]{:S(2)}) async-start(), calls=%async_computation | async-start | bytes 1114112 | tf_op jit(solution)/shard_map/all_gather | solution.py:87
  7.9 204.0 %all-gather.6.cloned.1.call-start = ((), (), s32[]{:S(2)}) async-start(), calls=%async_computation.1 | async-start | bytes 1114112 | tf_op jit(solution)/shard_map/all_gather | solution.py:88
  8.7 555.9 %all-reduce.3.cloned.1.call-start = ((), (), s32[]{:S(2)}) async-start(), calls=%async_computation.2 | async-start | bytes 3145728 | tf_op jit(solution)/shard_map/psum | solution.py:114
  114.6 3.7 copy-start.31
  145.3 7.6 %copy-start.17 = (bf16[64,128]{1,0:T(8,128)(2,1)S(1)}, bf16[64,128]{1,0:T(8,128)(2,1)}, u32[]{:S(2)}) copy-start(bf16[64,128]{1,0:T(8,128)(2,1)} %param.20) | copy-start | bytes 49156
  145.4 32.0 %copy-start.16 = (bf16[256,64]{0,1:T(8,128)(2,1)S(1)}, bf16[256,64]{0,1:T(8,128)(2,1)}, u32[]{:S(2)}) copy-start(bf16[256,64]{0,1:T(8,128)(2,1)} %param.19) | copy-start | bytes 98308
  145.7 59.9 %copy-start.5 = (bf16[4,64,1,2048]{3,1,2,0:T(8,128)(2,1)S(1)}, bf16[4,64,1,2048]{3,1,2,0:T(8,128)(2,1)}, u32[]{:S(2)}) copy-start(bf16[4,64,1,2048]{3,1,2,0:T(8,128)(2,1)} %param.12) | copy-start | bytes 3145732
  210.8 4.2 copy-start.10
  211.7 6.6 %copy-start.18 = (f32[256,4]{0,1:T(4,128)}, f32[256,4]{0,1:T(4,128)S(1)}, u32[]{:S(2)}) copy-start(f32[256,4]{0,1:T(4,128)S(1)} %fusion.2) | copy-start | bytes 12292
  216.4 5.6 copy-start.4
  222.0 3.1 copy-start.11
  232.1 3.1 copy-start.12
  242.3 3.1 copy-start.13
  246.9 4.8 copy-start.20
  246.9 4.8 copy-start.25
  251.7 4.8 copy-start.22
  251.7 4.8 copy-start.26
  256.5 4.8 copy-start.24
  256.5 4.8 copy-start.27
  266.2 3.7 copy-start.15
  266.2 3.7 copy-start.28
  266.2 3.7 copy-start.29
  266.2 3.7 copy-start.30
  (11 other events, 20.1 us)
Sparse Core Ops, SparseCore 0:
  10.1 66.9 all-gather.3
  79.2 69.6 all-gather.5
  272.2 292.3 all-reduce.2
where the time goes:
time: 575 us; the launch traced here: 574 us
  waiting for transfers between devices  294 us (51%)
  blocking collectives  182 us (32%)
  matrix products  45.8 us (8%)
  local copies, waits for them, and re-layouts  25.3 us (4%)
  between operations  14.1 us (2%)
  other arithmetic  13.1 us (2%)
    psum x1, waiting for transfers between devices, body(): down_sum, up_sum = lax.psum((down_term, up_term), ('dp', 'fsdp'))  293 us
    psum x1, blocking collectives, body(): seq_ratio = lax.psum(partial_value, ('dp', 'fsdp'))  105 us
    all_gather x1, blocking collectives, body(): lax.all_gather(adapter_down_factor, 'fsdp', axis=0, tiled=True)  27.5 us
    all_gather x1, blocking collectives, body(): lax.all_gather(attention_norm_gain, 'fsdp', axis=0, tiled=True)  24.8 us
    all_gather x1, blocking collectives, body(): lax.all_gather(adapter_up_factor, 'fsdp', axis=1, tiled=True)  24.4 us
    dot_general x4, matrix products, attend(): jnp.einsum('nhj,jd->nhd', grad_score, head_key, preferred_element_type=jn...  19.2 us
    dot_general x4, matrix products, attend(): jnp.einsum('nhj,jd->nhd', weights, head_value, preferred_element_type=jnp...  12.3 us
  transfers between devices with their start and end apart: 3, of which 1 were waited for; matrix products, arithmetic and copies ran while one was open for 3% of the time, Pallas kernels for 0%

commit v1 on v0

--- a/solution.py
+++ b/solution.py
@@ -3,6 +3,7 @@
 import jax.numpy as jnp
 from jax import lax
 from jax.sharding import PartitionSpec as P
+from jax.lax import psum
 
 HEAD_SIZE = 128
 QUERY_HEADS = 16
@@ -111,7 +112,7 @@
         query_gradient, up_full.T, preferred_element_type=jnp.float32
     ).astype(jnp.bfloat16)
     down_term = jnp.dot(normed_input.T, gradient_lowrank, preferred_element_type=jnp.float32)
-    down_sum, up_sum = lax.psum((down_term, up_term), ("dp", "fsdp"))
+    down_sum, up_sum = psum(psum((down_term, up_term), "fsdp"), "dp")
     down_factor_part = adapter_down_factor.shape[0]
     up_factor_part = adapter_up_factor.shape[1]
     grad_down = lax.dynamic_slice_in_dim(

time: 575 us -> 737 us (1.28)
  the two profiles are of different devices: /device:TPU:17 before, /device:TPU:1 now
where the time goes in v1:
time: 737 us; the launch traced here: 736 us
  waiting for transfers between devices  454 us (62%)
  blocking collectives  183 us (25%)
  matrix products  45.8 us (6%)
  local copies, waits for them, and re-layouts  25.2 us (3%)
  between operations  14.1 us (2%)
  other arithmetic  13.1 us (2%)
    psum x2, waiting for transfers between devices, body(): down_sum, up_sum = psum(psum((down_term, up_term), 'fsdp'), 'dp')  453 us
    psum x1, blocking collectives, body(): seq_ratio = lax.psum(partial_value, ('dp', 'fsdp'))  107 us
    all_gather x1, blocking collectives, body(): lax.all_gather(adapter_down_factor, 'fsdp', axis=0, tiled=True)  27.2 us
    all_gather x1, blocking collectives, body(): lax.all_gather(attention_norm_gain, 'fsdp', axis=0, tiled=True)  24.9 us
    all_gather x1, blocking collectives, body(): lax.all_gather(adapter_up_factor, 'fsdp', axis=1, tiled=True)  24 us
    dot_general x4, matrix products, attend(): jnp.einsum('nhj,jd->nhd', grad_score, head_key, preferred_element_type=jn...  19.2 us
  transfers between devices with their start and end apart: 4, of which 2 were waited for; matrix products, arithmetic and copies ran while one was open for 3% of the time, Pallas kernels for 0%

profile of v1, /device:TPU:1, one launch (start us, length us, event | category | flops | bytes accessed | tf_op | source)
XLA Modules:
  0.0 736.0 jit_solution(5776984234282004746)
XLA Ops:
  9.6 107.1 %psum.35 = f32[4]{0:T(128)S(1)} all-reduce(f32[4]{0:T(128)S(1)} %get-tuple-element.7), channel_id=1, replica_groups=mesh['dp'=32,'fsdp'=16] {'dp','fsdp'}, use_global_device_ids=true, to_apply=%region_4.5 | all-reduce | flops 4 | bytes 32 | tf_op jit(solution)/shard_map/psum | solution.py:80
  118.3 2.1 multiply_reduce_fusion
  120.5 24.9 %all-gather = bf16[16,1,256]{2,1,0:T(2,128)(2,1)S(1)} all-gather(bf16[1,1,256]{2,1,0:T(2,128)(2,1)S(1)} %reshape.122), channel_id=1, replica_groups=mesh['dp'=32,'fsdp'=16] {'fsdp'}, dimensions={0}, use_global_device_ids=true | all-gather | bytes 8704 | tf_op jit(solution)/shard_map/all_gather | solution.py:85
  145.4 2.2 fusion.1
  155.2 24.0 %all_gather.17 = bf16[64,2048]{1,0:T(8,128)(2,1)S(1)} all-gather(bf16[64,128]{1,0:T(8,128)(2,1)S(1)} %copy-done.17), channel_id=1, replica_groups=mesh['dp'=32,'fsdp'=16] {'fsdp'}, dimensions={1}, use_global_device_ids=true | all-gather | bytes 278528 | tf_op jit(solution)/shard_map/all_gather | solution.py:84
  179.2 27.2 %all_gather.16 = bf16[4096,64]{0,1:T(8,128)(2,1)S(1)} all-gather(bf16[256,64]{0,1:T(8,128)(2,1)S(1)} %copy-done.16), channel_id=1, replica_groups=mesh['dp'=32,'fsdp'=16] {'fsdp'}, dimensions={0}, use_global_device_ids=true | all-gather | bytes 557056 | tf_op jit(solution)/shard_map/all_gather | solution.py:83
  210.5 2.0 copy-done
  213.6 3.0 fusion.39
  218.1 1.9 multiply_reduce_fusion.1
  220.0 1.9 copy-done.1
  223.7 3.1 fusion.30
  230.0 1.9 copy-done.2
  233.7 3.1 fusion.33
  238.2 1.8 multiply_reduce_fusion.3
  240.1 1.9 copy-done.3
  243.9 3.1 fusion.36
  248.5 4.8 fusion.21
  253.3 4.8 fusion.24
  258.2 4.8 fusion.23
  263.0 4.8 fusion.22
  267.8 3.6 fusion.25
  271.4 2.2 fusion.70
  273.7 149.1 %all-reduce.7.cloned.1.call-done = (f32[4096,64]{0,1:T(8,128)}, f32[64,2048]{1,0:T(8,128)}) async-done(((f32[4096,64]{0,1:T(8,128)}, f32[64,2048]{1,0:T(8,128)}), (f32[4096,64]{0,1:T(8,128)}, f32[64,2048]{1,0:T(8,128)})) %all-reduce.7.cloned.1.call-update) | async-done | bytes 1572880 | tf_op jit(solution)/shard_map/psum | solution.py:115
  422.9 303.7 %all-reduce.5.cloned.1.call-done = (f32[4096,64]{0,1:T(8,128)}, f32[64,2048]{1,0:T(8,128)}) async-done(((f32[4096,64]{0,1:T(8,128)}, f32[64,2048]{1,0:T(8,128)}), (f32[4096,64]{0,1:T(8,128)}, f32[64,2048]{1,0:T(8,128)})) %all-reduce.5.cloned.1.call-update) | async-done | bytes 1572880 | tf_op jit(solution)/shard_map/psum | solution.py:115
  (109 shorter events, 32.7 us)
Async XLA Ops:
  7.2 140.4 %copy-start.6 = (bf16[4,64,1,2048]{3,1,2,0:T(8,128)(2,1)S(1)}, bf16[4,64,1,2048]{3,1,2,0:T(8,128)(2,1)}, u32[]{:S(2)}) copy-start(bf16[4,64,1,2048]{3,1,2,0:T(8,128)(2,1)} %param.13) | copy-start | bytes 3145732
  7.2 201.6 %all-gather.4.cloned.1.call-start = ((), (), s32[]{:S(2)}) async-start(), calls=%async_computation | async-start | bytes 1114112 | tf_op jit(solution)/shard_map/all_gather | solution.py:88
  7.9 205.7 %all-gather.6.cloned.1.call-start = ((), (), s32[]{:S(2)}) async-start(), calls=%async_computation.1 | async-start | bytes 1114112 | tf_op jit(solution)/shard_map/all_gather | solution.py:89
  8.7 414.2 %all-reduce.7.cloned.1.call-start = ((), (), s32[]{:S(2)}) async-start(), calls=%async_computation.3 | async-start | bytes 3145728 | tf_op jit(solution)/shard_map/psum | solution.py:115
  116.7 3.7 copy-start.31
  147.6 7.6 %copy-start.17 = (bf16[64,128]{1,0:T(8,128)(2,1)S(1)}, bf16[64,128]{1,0:T(8,128)(2,1)}, u32[]{:S(2)}) copy-start(bf16[64,128]{1,0:T(8,128)(2,1)} %param.20) | copy-start | bytes 49156
  147.6 31.6 %copy-start.16 = (bf16[256,64]{0,1:T(8,128)(2,1)S(1)}, bf16[256,64]{0,1:T(8,128)(2,1)}, u32[]{:S(2)}) copy-start(bf16[256,64]{0,1:T(8,128)(2,1)} %param.19) | copy-start | bytes 98308
  148.0 59.2 %copy-start.5 = (bf16[4,64,1,2048]{3,1,2,0:T(8,128)(2,1)S(1)}, bf16[4,64,1,2048]{3,1,2,0:T(8,128)(2,1)}, u32[]{:S(2)}) copy-start(bf16[4,64,1,2048]{3,1,2,0:T(8,128)(2,1)} %param.12) | copy-start | bytes 3145732
  212.5 4.2 copy-start.10
  213.4 6.6 copy-start.18
  218.1 5.6 copy-start.4
  223.7 3.1 copy-start.11
  243.9 3.1 copy-start.13
  248.5 4.8 copy-start.20
  248.5 4.8 copy-start.25
  253.3 4.8 copy-start.22
  253.3 4.8 copy-start.26
  258.1 4.8 copy-start.24
  258.1 4.8 copy-start.27
  267.8 3.7 copy-start.15
  267.8 3.7 copy-start.28
  267.8 3.7 copy-start.29
  267.8 3.7 copy-start.30
  273.7 453.0 %all-reduce.5.cloned.1.call-start = ((), (), s32[]{:S(2)}) async-start(), calls=%async_computation.2 | async-start | bytes 3145728 | tf_op jit(solution)/shard_map/psum | solution.py:115
  (12 other events, 23.2 us)
Sparse Core Ops, SparseCore 0:
  10.1 67.9 all-gather.3
  80.1 70.1 all-gather.5
  273.8 149.0 all-reduce.6
  426.0 300.6 all-reduce.4
